TPU v7x, 512 devices: a whole 4x4x16 slice. The times are simulated.
512 devices in a mesh: uly: 8 (over x_hi, y), blk: 64 (over z, x_lo, core).
Axes of the slice: x: 4 (x_hi: 2, x_lo: 2; x = x_hi * 2 + x_lo), y: 4, z: 16, core: 2. Of those that a mesh axis runs over, the one named last changes fastest.
Arguments:
- query: bfloat16 [131072, 1024], P(('uly', 'blk')), as said below
- key: bfloat16 [131072, 1024], P(('uly', 'blk')), as said below
- value: bfloat16 [131072, 1024], P(('uly', 'blk')), may hold values from -5 to 5
- live: int32 [8, 16, 64, 27], P('uly', None, 'blk'), may hold values from 0 to 1, as said below
Outputs:
- attended: bfloat16 [131072, 1024], P(('uly', 'blk'))
Inputs may be any that keep to these rules, and one draw needn't show every extreme that they name: `query`: entries lie within -5 to 5. `key`: entries lie within -5 to 5. live[h, f, s, 13] = 1 always; live is 0 for every neighbour that lies outside the grid of 16 x 8 x 8 tiles.
All inputs are finite; a program needn't handle non-finite values.
Results may differ from a plain program's by a relative error of at most 0.0046.
Values may be sent and summed in bfloat16 or wider, within the bound.
A program may use at most 128 MiB of HBM per device.

v0:
```python
import jax
import jax.numpy as jnp
from jax import lax
from jax.sharding import PartitionSpec as P

HD = 128
HEADS = 8
TILE = 128
TW = 8


def shifted(block, axis, distance):
    devices = range(lax.axis_size(axis))
    route = [(i - distance, i) for i in devices if i - distance in devices]
    return lax.ppermute(block, axis, route)


def local(query, key, value, live):
    uly_count = lax.axis_size("uly")
    tok_rows = query.shape[0]
    local_heads = HEADS // uly_count
    frames = uly_count * tok_rows // TILE
    scale = HD ** (-0.5)
    query_in, key_in, value_in = (
        lax.all_to_all(
            query.reshape(tok_rows, HEADS, HD), "uly", split_axis=1, concat_axis=0, tiled=True
        ),
        lax.all_to_all(
            key.reshape(tok_rows, HEADS, HD), "uly", split_axis=1, concat_axis=0, tiled=True
        ),
        lax.all_to_all(
            value.reshape(tok_rows, HEADS, HD), "uly", split_axis=1, concat_axis=0, tiled=True
        ),
    )
    query_tiles = query_in.reshape(frames, TILE, local_heads, HD)
    paired = jnp.stack(
        [
            key_in.reshape(frames, TILE, local_heads, HD),
            value_in.reshape(frames, TILE, local_heads, HD),
        ],
        axis=1,
    )
    pieces = []
    for row_step in (-1, 0, 1):
        for col_step in (-1, 0, 1):
            if row_step == 0 and col_step == 0:
                pieces.append(paired)
            else:
                pieces.append(shifted(paired, "blk", -(row_step * TW + col_step)))
    near = jnp.stack(pieces, axis=1).reshape((frames, 3, 3) + paired.shape[1:])
    padded = jnp.pad(near, ((1, 1),) + ((0, 0),) * (near.ndim - 1))
    allowed_all = live.reshape(local_heads, frames, 27)

    def one_frame(frame):
        block = lax.dynamic_slice_in_dim(padded, frame, 3, 0)
        keys_block = block[:, :, :, 0].reshape(27 * TILE, local_heads, HD)
        values_block = block[:, :, :, 1].reshape(27 * TILE, local_heads, HD)
        query_tile = lax.dynamic_index_in_dim(query_tiles, frame, 0, keepdims=False)
        scores = (
            jnp.einsum("qhd,khd->hqk", query_tile, keys_block, preferred_element_type=jnp.float32)
            * scale
        )
        allowed = lax.dynamic_index_in_dim(allowed_all, frame, 1, keepdims=False)
        allowed = jnp.repeat(allowed > 0, TILE, axis=1)[:, None, :]
        masked = jnp.where(allowed, scores, -1e30)
        top = jnp.max(masked, axis=2, keepdims=True)
        weights = jnp.where(allowed, jnp.exp(masked - top), 0.0)
        total = jnp.sum(weights, axis=2)
        mixed = jnp.einsum(
            "hqk,khd->qhd",
            weights.astype(jnp.bfloat16),
            values_block,
            preferred_element_type=jnp.float32,
        )
        return (mixed / jnp.transpose(total)[:, :, None]).astype(jnp.bfloat16)

    outputs = lax.map(one_frame, jnp.arange(frames))
    returned = lax.all_to_all(
        outputs.reshape(uly_count * tok_rows, local_heads, HD),
        "uly",
        split_axis=0,
        concat_axis=1,
        tiled=True,
    )
    return returned.reshape(tok_rows, HEADS * HD)


def solution(mesh):
    return jax.shard_map(
        local,
        mesh=mesh,
        in_specs=(
            P(("uly", "blk"), None),
            P(("uly", "blk"), None),
            P(("uly", "blk"), None),
            P("uly", None, "blk", None),
        ),
        out_specs=P(("uly", "blk"), None),
        check_vma=False,
    )
```

profile of v0, /device:TPU:96, one launch (start us, length us, event | category | flops | bytes accessed | tf_op | source)
XLA Modules:
  0.0 426.8 jit_solution(10464731369416889189)
XLA Ops:
  1.9 6.9 %all-to-all-start = ((bf16[256,8,128]{2,0,1:T(8,128)(2,1)}), bf16[256,8,128]{2,0,1:T(8,128)(2,1)S(1)}, u32[]{:S(2)}, u32[]{:S(2)}) async-start(bf16[256,8,128]{2,0,1:T(8,128)(2,1)} %copy_bitcast_fusion.1), calls=%async_computation | async-start | bytes 1048576 | tf_op jit(solution)/shard_map/all_to_all | solution.py:28
  10.0 9.9 %all-to-all-done = bf16[256,8,128]{2,0,1:T(8,128)(2,1)S(1)} async-done(((bf16[256,8,128]{2,0,1:T(8,128)(2,1)}), bf16[256,8,128]{2,0,1:T(8,128)(2,1)S(1)}, u32[]{:S(2)}, u32[]{:S(2)}) %all-to-all-start) | async-done | bytes 524320 | tf_op jit(solution)/shard_map/all_to_all | solution.py:28
  19.9 14.8 %all_to_all.60 = bf16[256,8,128]{2,0,1:T(8,128)(2,1)S(1)} all-to-all(bf16[256,8,128]{2,0,1:T(8,128)(2,1)S(1)} %copy_bitcast_fusion), channel_id=1, replica_groups=mesh['uly'=8,'blk'=64] {'uly'}, dimensions={1} | all-to-all | bytes 1048576 | tf_op jit(solution)/shard_map/all_to_all | solution.py:31
  34.8 4.1 collective-permute-start
  38.9 5.2 %collective-permute-start.1 = (bf16[16,2,128,1,128]{4,2,1,0,3:T(8,128)(2,1)S(1)}, bf16[16,2,128,1,128]{4,2,1,0,3:T(8,128)(2,1)}, u32[]{:S(2)}, u32[]{:S(2)}) collective-permute-start(bf16[16,2,128,1,128]{4,2,1,0,3:T(8,128)(2,1)S(1)} %pad_maximum_fusion), channel_id=1, source_target_pairs={{0,8},{1,9},{2,10},{3,11},{4,12},{5,13},{6,14},{7,15},{8,16},{9,17... | collective-permute-start | bytes 3145736 | tf_op jit(solution)/shard_map/ppermute | solution.py:15
  44.0 8.2 %collective-permute-start.2 = (bf16[16,2,128,1,128]{4,2,1,0,3:T(8,128)(2,1)S(1)}, bf16[16,2,128,1,128]{4,2,1,0,3:T(8,128)(2,1)}, u32[]{:S(2)}, u32[]{:S(2)}) collective-permute-start(bf16[16,2,128,1,128]{4,2,1,0,3:T(8,128)(2,1)S(1)} %pad_maximum_fusion), channel_id=1, source_target_pairs={{0,7},{1,8},{2,9},{3,10},{4,11},{5,12},{6,13},{7,14},{8,15},{9,16}... | collective-permute-start | bytes 3145736 | tf_op jit(solution)/shard_map/ppermute | solution.py:15
  52.2 2.1 copy.56
  54.3 3.5 all-to-all-start.2
  57.8 1.9 collective-permute-start.3
  59.7 4.5 %collective-permute-start.4 = (bf16[16,2,128,1,128]{4,2,1,0,3:T(8,128)(2,1)S(1)}, bf16[16,2,128,1,128]{4,2,1,0,3:T(8,128)(2,1)}, u32[]{:S(2)}, u32[]{:S(2)}) collective-permute-start(bf16[16,2,128,1,128]{4,2,1,0,3:T(8,128)(2,1)S(1)} %pad_maximum_fusion), channel_id=1, source_target_pairs={{1,0},{2,1},{3,2},{4,3},{5,4},{6,5},{7,6},{8,7},{9,8},{10,9},{11,1... | collective-permute-start | bytes 3145736 | tf_op jit(solution)/shard_map/ppermute | solution.py:15
  64.3 3.2 all-to-all-done.2
  68.5 42.0 %collective-permute-done = bf16[16,2,128,1,128]{4,2,1,0,3:T(8,128)(2,1)} collective-permute-done((bf16[16,2,128,1,128]{4,2,1,0,3:T(8,128)(2,1)S(1)}, bf16[16,2,128,1,128]{4,2,1,0,3:T(8,128)(2,1)}, u32[]{:S(2)}, u32[]{:S(2)}) %collective-permute-start) | collective-permute-done | bytes 1048608 | tf_op jit(solution)/shard_map/ppermute | solution.py:15
  110.5 7.8 %collective-permute-start.5 = (bf16[16,2,128,1,128]{4,2,1,0,3:T(8,128)(2,1)S(1)}, bf16[16,2,128,1,128]{4,2,1,0,3:T(8,128)(2,1)S(1)}, u32[]{:S(2)}, u32[]{:S(2)}) collective-permute-start(bf16[16,2,128,1,128]{4,2,1,0,3:T(8,128)(2,1)S(1)} %pad_maximum_fusion), channel_id=1, source_target_pairs={{7,0},{8,1},{9,2},{10,3},{11,4},{12,5},{13,6},{14,7},{15,8},{16,9}... | collective-permute-start | bytes 3145736 | tf_op jit(solution)/shard_map/ppermute | solution.py:15
  118.3 2.5 bitcast_dynamic-update-slice_fusion.7
  120.8 18.7 %collective-permute-done.1 = bf16[16,2,128,1,128]{4,2,1,0,3:T(8,128)(2,1)} collective-permute-done((bf16[16,2,128,1,128]{4,2,1,0,3:T(8,128)(2,1)S(1)}, bf16[16,2,128,1,128]{4,2,1,0,3:T(8,128)(2,1)}, u32[]{:S(2)}, u32[]{:S(2)}) %collective-permute-start.1) | collective-permute-done | bytes 1048608 | tf_op jit(solution)/shard_map/ppermute | solution.py:15
  139.6 1.9 collective-permute-start.6
  141.5 2.5 bitcast_dynamic-update-slice_fusion.6
  144.0 18.1 %collective-permute-done.2 = bf16[16,2,128,1,128]{4,2,1,0,3:T(8,128)(2,1)} collective-permute-done((bf16[16,2,128,1,128]{4,2,1,0,3:T(8,128)(2,1)S(1)}, bf16[16,2,128,1,128]{4,2,1,0,3:T(8,128)(2,1)}, u32[]{:S(2)}, u32[]{:S(2)}) %collective-permute-start.2) | collective-permute-done | bytes 1048608 | tf_op jit(solution)/shard_map/ppermute | solution.py:15
  162.1 1.9 collective-permute-start.7
  164.0 2.6 bitcast_dynamic-update-slice_fusion.5
  166.6 33.1 %collective-permute-done.3 = bf16[16,2,128,1,128]{4,2,1,0,3:T(8,128)(2,1)} collective-permute-done((bf16[16,2,128,1,128]{4,2,1,0,3:T(8,128)(2,1)S(1)}, bf16[16,2,128,1,128]{4,2,1,0,3:T(8,128)(2,1)}, u32[]{:S(2)}, u32[]{:S(2)}) %collective-permute-start.3) | collective-permute-done | bytes 1048608 | tf_op jit(solution)/shard_map/ppermute | solution.py:15
  199.6 2.6 bitcast_dynamic-update-slice_fusion.4
  203.4 2.5 bitcast_dynamic-update-slice_fusion.2
  208.4 50.6 %collective-permute-done.7 = bf16[16,2,128,1,128]{4,2,1,0,3:T(8,128)(2,1)S(1)} collective-permute-done((bf16[16,2,128,1,128]{4,2,1,0,3:T(8,128)(2,1)S(1)}, bf16[16,2,128,1,128]{4,2,1,0,3:T(8,128)(2,1)S(1)}, u32[]{:S(2)}, u32[]{:S(2)}) %collective-permute-start.7) | collective-permute-done | bytes 1048608 | tf_op jit(solution)/shard_map/ppermute | solution.py:15
  260.2 12.3 %pad.4 = bf16[18,3,3,2,128,1,128]{6,4,3,2,1,0,5:T(8,128)(2,1)} pad(bf16[16,3,3,2,128,1,128]{6,4,3,2,1,0,5:T(8,128)(2,1)} %bitcast.32, bf16[]{:T(256)} %constant.32.clone.1), padding=1_1x0_0x0_0x0_0x0_0x0_0x0_0 | pad | bytes 20054018 | tf_op jit(solution)/shard_map/jit(_pad)/pad | solution.py:51
  272.5 137.1 %while.10 = (s32[]{:T(128)}, bf16[16,128,1,128]{3,1,0,2:T(8,128)(2,1)S(1)}, s32[16]{0:T(128)S(1)}, bf16[18,3,3,2,128,1,128]{6,4,3,2,1,0,5:T(8,128)(2,1)}, s32[1,...) while((s32[]{:T(128)}, ...), condition=%wide.region_3.4_spmd, body=%wide.region_0.3_spmd.sunk | while | flops 230506272 | bytes 10830198 | solution.py:77
  277.1 1.6 constant_dynamic-slice_fusion.4
  285.6 1.6 constant_dynamic-slice_fusion.4
  294.2 1.6 constant_dynamic-slice_fusion.4
  311.4 1.6 constant_dynamic-slice_fusion.4
  319.9 1.6 constant_dynamic-slice_fusion.4
  411.3 13.6 %all_to_all.61 = bf16[8,2,16384]{2,1,0:T(2,128)(2,1)S(1)} all-to-all(bf16[8,2,16384]{2,1,0:T(2,128)(2,1)S(1)} %reshape.81), channel_id=1, replica_groups=mesh['uly'=8,'blk'=64] {'uly'}, dimensions={0} | all-to-all | bytes 1048576 | tf_op jit(solution)/shard_map/all_to_all | solution.py:78
  (163 shorter events, 89.3 us)
Async XLA Ops:
  0.0 1.0 copy-start
  1.9 18.0 %all-to-all-start = ((bf16[256,8,128]{2,0,1:T(8,128)(2,1)}), bf16[256,8,128]{2,0,1:T(8,128)(2,1)S(1)}, u32[]{:S(2)}, u32[]{:S(2)}) async-start(bf16[256,8,128]{2,0,1:T(8,128)(2,1)} %copy_bitcast_fusion.1), calls=%async_computation | async-start | bytes 1048576 | tf_op jit(solution)/shard_map/all_to_all | solution.py:28
  34.8 75.7 %collective-permute-start = (bf16[16,2,128,1,128]{4,2,1,0,3:T(8,128)(2,1)S(1)}, bf16[16,2,128,1,128]{4,2,1,0,3:T(8,128)(2,1)}, u32[]{:S(2)}, u32[]{:S(2)}) collective-permute-start(bf16[16,2,128,1,128]{4,2,1,0,3:T(8,128)(2,1)S(1)} %pad_maximum_fusion), channel_id=1, source_target_pairs={{0,9},{1,10},{2,11},{3,12},{4,13},{5,14},{6,15},{7,16},{8,17},{9,1... | collective-permute-start | bytes 3145736 | tf_op jit(solution)/shard_map/ppermute | solution.py:15
  38.9 100.7 %collective-permute-start.1 = (bf16[16,2,128,1,128]{4,2,1,0,3:T(8,128)(2,1)S(1)}, bf16[16,2,128,1,128]{4,2,1,0,3:T(8,128)(2,1)}, u32[]{:S(2)}, u32[]{:S(2)}) collective-permute-start(bf16[16,2,128,1,128]{4,2,1,0,3:T(8,128)(2,1)S(1)} %pad_maximum_fusion), channel_id=1, source_target_pairs={{0,8},{1,9},{2,10},{3,11},{4,12},{5,13},{6,14},{7,15},{8,16},{9,17... | collective-permute-start | bytes 3145736 | tf_op jit(solution)/shard_map/ppermute | solution.py:15
  44.0 118.1 %collective-permute-start.2 = (bf16[16,2,128,1,128]{4,2,1,0,3:T(8,128)(2,1)S(1)}, bf16[16,2,128,1,128]{4,2,1,0,3:T(8,128)(2,1)}, u32[]{:S(2)}, u32[]{:S(2)}) collective-permute-start(bf16[16,2,128,1,128]{4,2,1,0,3:T(8,128)(2,1)S(1)} %pad_maximum_fusion), channel_id=1, source_target_pairs={{0,7},{1,8},{2,9},{3,10},{4,11},{5,12},{6,13},{7,14},{8,15},{9,16}... | collective-permute-start | bytes 3145736 | tf_op jit(solution)/shard_map/ppermute | solution.py:15
  54.3 13.2 %all-to-all-start.2 = ((bf16[256,8,128]{0,2,1:T(8,128)(2,1)}), bf16[256,8,128]{0,2,1:T(8,128)(2,1)S(1)}, u32[]{:S(2)}, u32[]{:S(2)}) async-start(bf16[256,8,128]{0,2,1:T(8,128)(2,1)} %bitcast.34), calls=%async_computation.2 | async-start | bytes 1048576 | tf_op jit(solution)/shard_map/all_to_all | solution.py:25
  57.8 141.8 %collective-permute-start.3 = (bf16[16,2,128,1,128]{4,2,1,0,3:T(8,128)(2,1)S(1)}, bf16[16,2,128,1,128]{4,2,1,0,3:T(8,128)(2,1)}, u32[]{:S(2)}, u32[]{:S(2)}) collective-permute-start(bf16[16,2,128,1,128]{4,2,1,0,3:T(8,128)(2,1)S(1)} %pad_maximum_fusion), channel_id=1, source_target_pairs={{0,1},{1,2},{2,3},{3,4},{4,5},{5,6},{6,7},{7,8},{8,9},{9,10},{10,1... | collective-permute-start | bytes 3145736 | tf_op jit(solution)/shard_map/ppermute | solution.py:15
  59.7 143.7 %collective-permute-start.4 = (bf16[16,2,128,1,128]{4,2,1,0,3:T(8,128)(2,1)S(1)}, bf16[16,2,128,1,128]{4,2,1,0,3:T(8,128)(2,1)}, u32[]{:S(2)}, u32[]{:S(2)}) collective-permute-start(bf16[16,2,128,1,128]{4,2,1,0,3:T(8,128)(2,1)S(1)} %pad_maximum_fusion), channel_id=1, source_target_pairs={{1,0},{2,1},{3,2},{4,3},{5,4},{6,5},{7,6},{8,7},{9,8},{10,9},{11,1... | collective-permute-start | bytes 3145736 | tf_op jit(solution)/shard_map/ppermute | solution.py:15
  110.5 95.4 %collective-permute-start.5 = (bf16[16,2,128,1,128]{4,2,1,0,3:T(8,128)(2,1)S(1)}, bf16[16,2,128,1,128]{4,2,1,0,3:T(8,128)(2,1)S(1)}, u32[]{:S(2)}, u32[]{:S(2)}) collective-permute-start(bf16[16,2,128,1,128]{4,2,1,0,3:T(8,128)(2,1)S(1)} %pad_maximum_fusion), channel_id=1, source_target_pairs={{7,0},{8,1},{9,2},{10,3},{11,4},{12,5},{13,6},{14,7},{15,8},{16,9}... | collective-permute-start | bytes 3145736 | tf_op jit(solution)/shard_map/ppermute | solution.py:15
  139.6 67.6 %collective-permute-start.6 = (bf16[16,2,128,1,128]{4,2,1,0,3:T(8,128)(2,1)S(1)}, bf16[16,2,128,1,128]{4,2,1,0,3:T(8,128)(2,1)S(1)}, u32[]{:S(2)}, u32[]{:S(2)}) collective-permute-start(bf16[16,2,128,1,128]{4,2,1,0,3:T(8,128)(2,1)S(1)} %pad_maximum_fusion), channel_id=1, source_target_pairs={{8,0},{9,1},{10,2},{11,3},{12,4},{13,5},{14,6},{15,7},{16,8},{17,9... | collective-permute-start | bytes 3145736 | tf_op jit(solution)/shard_map/ppermute | solution.py:15
  162.1 96.9 %collective-permute-start.7 = (bf16[16,2,128,1,128]{4,2,1,0,3:T(8,128)(2,1)S(1)}, bf16[16,2,128,1,128]{4,2,1,0,3:T(8,128)(2,1)S(1)}, u32[]{:S(2)}, u32[]{:S(2)}) collective-permute-start(bf16[16,2,128,1,128]{4,2,1,0,3:T(8,128)(2,1)S(1)} %pad_maximum_fusion), channel_id=1, source_target_pairs={{9,0},{10,1},{11,2},{12,3},{13,4},{14,5},{15,6},{16,7},{17,8},{18,... | collective-permute-start | bytes 3145736 | tf_op jit(solution)/shard_map/ppermute | solution.py:15
  260.2 12.3 %copy-start.1 = (bf16[16,128,1,128]{3,1,0,2:T(8,128)(2,1)S(1)}, bf16[16,128,1,128]{3,1,0,2:T(8,128)(2,1)}, u32[]{:S(2)}) copy-start(bf16[16,128,1,128]{3,1,0,2:T(8,128)(2,1)} %custom-call.1) | copy-start | bytes 1572868
where the time goes:
time: 430 us; the launch traced here: 427 us
  waiting for transfers between devices  176 us (41%)
  local copies, waits for them, and re-layouts  74.9 us (17%)
  loops' own time  52.5 us (12%)
  starting transfers between devices  45.9 us (11%)
  blocking collectives  28.4 us (7%)
  matrix products  28.2 us (7%)
  other arithmetic  21.1 us (5%)
    ppermute x8, waiting for transfers between devices, shifted(): return lax.ppermute(block, axis, route)  162 us
    another operation x1, loops' own time, local(): outputs = lax.map(one_frame, jnp.arange(frames))  52.5 us
    ppermute x8, starting transfers between devices, shifted(): return lax.ppermute(block, axis, route)  35.5 us
    slice x16, local copies, waits for them, and re-layouts, one_frame(): keys_block = block[:, :, :, 0].reshape(27 * TILE, local_heads, HD)  25 us
    dot_general x16, matrix products, one_frame(): jnp.einsum('qhd,khd->hqk', query_tile, keys_block, preferred_element_type...  19.9 us
    unnamed x15, local copies, waits for them, and re-layouts  19 us
    all_to_all x1, blocking collectives, local(): lax.all_to_all(value.reshape(tok_rows, HEADS, HD), 'uly', split_axis=1, c...  14.8 us
    all_to_all x1, blocking collectives, local(): lax.all_to_all(outputs.reshape(uly_count * tok_rows, local_heads, HD), 'u...  13.6 us
  transfers between devices with their start and end apart: 10, of which 7 were waited for; matrix products, arithmetic and copies ran while one was open for 5% of the time, Pallas kernels for 0%

commit v1 on v0

v1 whole, which is shorter than its diff:
```python
import math

import jax
import jax.numpy as jnp
from jax import lax
from jax.experimental import pallas as pl
from jax.experimental.pallas import tpu as pltpu
from jax.sharding import PartitionSpec as P

HD = 128
TILE = 128
TW = 8
TH = 8
N = 8
FRAMES = 2 * N
LAG_V = 1
LAG_H = 2
LOGIT = HD ** (-0.5) * math.log2(math.e)
NEG = -1e30
MESH = pl.DeviceIdType.MESH
DMA = pltpu.SemaphoreType.DMA


def kernel(
    q_hbm, k_hbm, v_hbm, live, out_hbm,
    kv, qb, ob, sc,
    a_send, a_recv, v_send, v_recv, h_send, h_recv, o_send, o_recv,
):
    u = lax.axis_index("uly")
    s = lax.axis_index("blk")
    h = s // TW
    w = s % TW
    up = ((h + 1) % TH) * TW + w
    down = ((h + TH - 1) % TH) * TW + w
    right = h * TW + (w + 1) % TW
    left = h * TW + (w + TW - 1) % TW
    has_up, has_down = h < TH - 1, h > 0
    has_right, has_left = w < TW - 1, w > 0
    has_row = (has_down, None, has_up)

    barrier = pltpu.get_barrier_semaphore()
    for i in range(1, N):
        pl.semaphore_signal(barrier, inc=1, device_id=((u + i) % N, s), device_id_type=MESH)
    for other in (up, down, left, right):
        pl.semaphore_signal(barrier, inc=1, device_id=(u, other), device_id_type=MESH)
    pl.semaphore_wait(barrier, N + 3)

    def columns(ref, head):
        return ref.at[:, pl.ds(pl.multiple_of(head * HD, HD), HD)]

    def a_dst(x, chunk):
        return qb.at[chunk] if x == 2 else kv.at[1, 1, chunk, x]

    def a_copy(x, to, chunk):
        ref = (k_hbm, v_hbm, q_hbm)[x]
        return pltpu.make_async_remote_copy(
            src_ref=columns(ref, to), dst_ref=a_dst(x, chunk),
            send_sem=a_send.at[x, to], recv_sem=a_recv.at[x, chunk],
            device_id=(to, s), device_id_type=MESH)

    def a_own(x):
        ref = (k_hbm, v_hbm, q_hbm)[x]
        return pltpu.make_async_copy(columns(ref, u), a_dst(x, u), a_recv.at[x, u])

    for x in (0, 1, 2):
        a_own(x).start()
    for xs in ((0, 1), (2,)):
        @pl.loop(1, N)
        def _(i):
            to = (u + N - i) % N
            for x in xs:
                a_copy(x, to, u).start()

    def v_copy(d, chunk):
        return pltpu.make_async_remote_copy(
            src_ref=kv.at[1, 1, chunk], dst_ref=kv.at[1, 0 if d == 0 else 2, chunk],
            send_sem=v_send.at[d, chunk], recv_sem=v_recv.at[d, chunk],
            device_id=(u, up if d == 0 else down), device_id_type=MESH)

    def h_copy(d, r, chunk):
        return pltpu.make_async_remote_copy(
            src_ref=kv.at[1, r, chunk], dst_ref=kv.at[0 if d == 0 else 2, r, chunk],
            send_sem=h_send.at[d, r, chunk], recv_sem=h_recv.at[d, r, chunk],
            device_id=(u, right if d == 0 else left), device_id_type=MESH)

    def o_dst(frame, head):
        return out_hbm.at[pl.ds(pl.multiple_of(frame % 2 * TILE, TILE), TILE),
                          pl.ds(pl.multiple_of(head * HD, HD), HD)]

    def o_copy(frame):
        return pltpu.make_async_remote_copy(
            src_ref=ob.at[frame], dst_ref=o_dst(frame, u),
            send_sem=o_send.at[frame], recv_sem=o_recv.at[u, frame % 2],
            device_id=(frame // 2, s), device_id_type=MESH)

    def o_own(frame):
        return pltpu.make_async_copy(ob.at[frame], o_dst(frame, u), o_send.at[frame])

    def zero(*at):
        @pl.loop(0, N)
        def _(g):
            for part in range(2):
                kv[(*at, g, part)] = jnp.zeros((2 * TILE, HD), jnp.bfloat16)

    for missing, spots in (
        (h == 0, [(c, 0) for c in range(3)]),
        (h == TH - 1, [(c, 2) for c in range(3)]),
        (w == 0, [(0, r) for r in range(3)]),
        (w == TW - 1, [(2, r) for r in range(3)]),
    ):
        @pl.when(missing)
        def _():
            for spot in spots:
                zero(*spot)

    def attend(f):
        q = qb[f // 2, pl.ds(pl.multiple_of(f % 2 * TILE, TILE), TILE), :]
        spots = []
        for a in range(3):
            g = (f + a + FRAMES - 1) % FRAMES
            spots.append((g // 2, pl.multiple_of(g % 2 * TILE, TILE)))

        def near(c, r, part):
            return jnp.concatenate(
                [kv[c, r, g, part, pl.ds(off, TILE), :] for g, off in spots], axis=0)

        top = jnp.full((TILE, TILE), NEG, jnp.float32)
        for r in range(3):
            for c in range(3):
                scores = lax.dot_general(
                    q, near(c, r, 0), (((1,), (1,)), ((), ())),
                    preferred_element_type=jnp.float32)
                for a in range(3):
                    bias = jnp.where(live[f * 27 + 9 * a + 3 * r + c] > 0, 0.0, NEG)
                    part = scores[:, a * TILE:(a + 1) * TILE] * LOGIT + bias
                    sc[3 * r + c, :, a * TILE:(a + 1) * TILE] = part
                    top = jnp.maximum(top, part)
        top = jnp.max(top, axis=1, keepdims=True)
        total = jnp.zeros((TILE, TILE), jnp.float32)
        mixed = jnp.zeros((TILE, HD), jnp.float32)
        for r in range(3):
            for c in range(3):
                weights = jnp.exp2(sc[3 * r + c] - top)
                for a in range(3):
                    total += weights[:, a * TILE:(a + 1) * TILE]
                mixed += jnp.dot(
                    weights.astype(jnp.bfloat16), near(c, r, 1),
                    preferred_element_type=jnp.float32)
        ob[f] = (mixed / jnp.sum(total, axis=1, keepdims=True)).astype(jnp.bfloat16)

    def attend_and_send(f):
        attend(f)

        @pl.when(f // 2 == u)
        def _():
            o_own(f).start()

        @pl.when(f // 2 != u)
        def _():
            o_copy(f).start()

    def unit(c):
        @pl.loop(0, 2)
        def _(j):
            attend_and_send((2 * c + j + FRAMES - 1) % FRAMES)

    def wait_a(x, chunk):
        pltpu.make_async_copy(columns(k_hbm, 0), a_dst(x, chunk), a_recv.at[x, chunk]).wait()

    @pl.loop(0, N + LAG_H)
    def _(i):
        @pl.when(i < N)
        def _():
            c = (u + i) % N
            wait_a(0, c)
            wait_a(1, c)

            @pl.when(has_up)
            def _():
                v_copy(0, c).start()

            @pl.when(has_down)
            def _():
                v_copy(1, c).start()

            @pl.when(has_right)
            def _():
                h_copy(0, 1, c).start()

            @pl.when(has_left)
            def _():
                h_copy(1, 1, c).start()

        @pl.when((i >= LAG_V) & (i < N + LAG_V))
        def _():
            c = (u + i + N - LAG_V) % N
            for d, r, there in ((0, 0, has_down), (1, 2, has_up)):
                @pl.when(there)
                def _():
                    v_copy(d, c).wait_recv()

                    @pl.when(has_right)
                    def _():
                        h_copy(0, r, c).start()

                    @pl.when(has_left)
                    def _():
                        h_copy(1, r, c).start()

        @pl.when(i >= LAG_H)
        def _():
            c = (u + i + N - LAG_H) % N
            for d, there in ((0, has_left), (1, has_right)):
                for r in range(3):
                    here = there if r == 1 else there & has_row[r]

                    @pl.when(here)
                    def _():
                        h_copy(d, r, c).wait_recv()
            wait_a(2, c)

            @pl.when(i > LAG_H)
            def _():
                unit(c)

    unit(u)

    @pl.loop(0, N)
    def _(g):
        @pl.when(has_up)
        def _():
            v_copy(0, g).wait_send()

        @pl.when(has_down)
        def _():
            v_copy(1, g).wait_send()

        for d, there in ((0, has_right), (1, has_left)):
            for r in range(3):
                here = there if r == 1 else there & has_row[r]

                @pl.when(here)
                def _():
                    h_copy(d, r, g).wait_send()

        @pl.when(g != u)
        def _():
            for x in range(3):
                a_copy(x, g, u).wait_send()
            for j in range(2):
                o_copy(2 * g + j).wait_send()
                pltpu.make_async_copy(ob.at[j], o_dst(j, g), o_recv.at[g, j]).wait()

        @pl.when(g == u)
        def _():
            for j in range(2):
                o_own(2 * g + j).wait()


def local(query, key, value, live):
    rows, width = query.shape
    hbm = pl.BlockSpec(memory_space=pl.ANY)
    return pl.pallas_call(
        kernel,
        out_shape=jax.ShapeDtypeStruct((rows, width), jnp.bfloat16),
        in_specs=[hbm, hbm, hbm, pl.BlockSpec(memory_space=pltpu.SMEM)],
        out_specs=hbm,
        scratch_shapes=[
            pltpu.VMEM((3, 3, N, 2, 2 * TILE, HD), jnp.bfloat16),
            pltpu.VMEM((N, 2 * TILE, HD), jnp.bfloat16),
            pltpu.VMEM((FRAMES, TILE, HD), jnp.bfloat16),
            pltpu.VMEM((9, TILE, 3 * TILE), jnp.float32),
            DMA((3, N)), DMA((3, N)),
            DMA((2, N)), DMA((2, N)),
            DMA((2, 3, N)), DMA((2, 3, N)),
            DMA((FRAMES,)), DMA((N, 2)),
        ],
        compiler_params=pltpu.CompilerParams(
            collective_id=0, has_side_effects=True, vmem_limit_bytes=48 << 20),
    )(query, key, value, live.reshape(-1))


def solution(mesh):
    return jax.shard_map(
        local,
        mesh=mesh,
        in_specs=(
            P(("uly", "blk"), None),
            P(("uly", "blk"), None),
            P(("uly", "blk"), None),
            P("uly", None, "blk", None),
        ),
        out_specs=P(("uly", "blk"), None),
        check_vma=False,
    )
```

time: 430 us -> 112 us (0.26)
  the two profiles are of different devices: /device:TPU:96 before, /device:TPU:113 now
where the time goes in v1:
time: 112 us; the launch traced here: 111 us
  Pallas kernels  106 us (95%)
  local copies, waits for them, and re-layouts  4.51 us (4%)
  other arithmetic  1.37 us (1%)
    pallas_call x1, Pallas kernels, local(): pl.pallas_call(kernel, out_shape=jax.ShapeDtypeStruct((rows, width), jnp....  106 us
    unnamed x8, local copies, waits for them, and re-layouts  4.43 us

profile of v1, /device:TPU:113, one launch (start us, length us, event | category | flops | bytes accessed | tf_op | source)
XLA Modules:
  0.0 111.5 jit_solution(7054272071897480748)
XLA Ops:
  0.0 0.5 broadcast.3
  0.5 1.4 %reduce.3 = s32[16,27]{1,0:T(8,128)S(1)} reduce(s32[1,16,1,27]{3,2,1,0:T(1,128)} %param.7, s32[]{:T(128)} %broadcast.3), dimensions={0,2}, to_apply=%param.7.reduce_sub_computation.3 | reduce | bytes 3460 | tf_op args[3]
  1.9 0.1 reshape.3.live
  2.0 0.0 copy-start
  2.0 1.0 copy-done
  3.0 0.0 copy-start.1
  3.0 1.0 copy-done.1
  4.1 0.0 copy-start.2
  4.1 1.0 copy-done.2
  5.1 105.6 %shard_map.46 = bf16[256,1024]{1,0:T(8,128)(2,1)S(1)} custom-call(bf16[256,1024]{1,0:T(8,128)(2,1)S(1)} %copy-done, bf16[256,1024]{1,0:T(8,128)(2,1)S(1)} %copy-done.1, bf16[256,1024]{1,0:T(8,128)(2,1)S(1)} %copy-done.2, s32[432]{0:T(512)S(1)} %reshape.3.live), custom_call_target="tpu_custom_call" | custom-call | tf_op jit(solution)/shard_map/pallas_call | solution.py:263
  110.7 0.8 copy.6
Async XLA Ops:
  2.0 1.0 copy-start
  3.0 1.0 copy-start.1
  4.1 1.0 copy-start.2

commit v2 on v1

--- a/solution.py
+++ b/solution.py
@@ -1,3 +1,4 @@
+import functools
 import math
 
 import jax
@@ -14,7 +15,8 @@
 N = 8
 FRAMES = 2 * N
 LAG_V = 1
-LAG_H = 2
+LAG_R = 2
+LAG_H = 3
 LOGIT = HD ** (-0.5) * math.log2(math.e)
 NEG = -1e30
 MESH = pl.DeviceIdType.MESH
@@ -23,8 +25,8 @@
 
 def kernel(
     q_hbm, k_hbm, v_hbm, live, out_hbm,
-    kv, qb, ob, sc,
-    a_send, a_recv, v_send, v_recv, h_send, h_recv, o_send, o_recv,
+    kv, qb, ob, sc, passing,
+    a_send, a_recv, v_send, v_recv, h_send, h_recv, c_send, c_recv, r_send, r_recv, o_send, o_recv,
 ):
     u = lax.axis_index("uly")
     s = lax.axis_index("blk")
@@ -37,13 +39,27 @@
     has_up, has_down = h < TH - 1, h > 0
     has_right, has_left = w < TW - 1, w > 0
     has_row = (has_down, None, has_up)
+    crosses = (w == 3) | (w == 4)
+    relays = (w == 1) | (w == 6)
+    relay = h * TW + jnp.where(w == 3, 1, 6)
+    beyond = h * TW + jnp.where(w == 1, 4, 3)
+    beyond_column = jnp.where(w == 1, 0, 2)
+    far_column = jnp.where(w == 3, 2, 0)
 
     barrier = pltpu.get_barrier_semaphore()
     for i in range(1, N):
         pl.semaphore_signal(barrier, inc=1, device_id=((u + i) % N, s), device_id_type=MESH)
     for other in (up, down, left, right):
         pl.semaphore_signal(barrier, inc=1, device_id=(u, other), device_id_type=MESH)
-    pl.semaphore_wait(barrier, N + 3)
+    extra = crosses | relays
+
+    @pl.when(extra)
+    def _():
+        for a, b in ((1, 3), (6, 4)):
+            other = h * TW + jnp.where(crosses, a, b)
+            pl.semaphore_signal(barrier, inc=1, device_id=(u, other), device_id_type=MESH)
+
+    pl.semaphore_wait(barrier, N + 3 + 2 * extra.astype(jnp.int32))
 
     def columns(ref, head):
         return ref.at[:, pl.ds(pl.multiple_of(head * HD, HD), HD)]
@@ -83,6 +99,80 @@
             send_sem=h_send.at[d, r, chunk], recv_sem=h_recv.at[d, r, chunk],
             device_id=(u, right if d == 0 else left), device_id_type=MESH)
 
+    def near_half(d, r, chunk):
+        return pltpu.make_async_remote_copy(
+            src_ref=kv.at[1, r, chunk, 0], dst_ref=kv.at[0 if d == 0 else 2, r, chunk, 0],
+            send_sem=h_send.at[d, r, chunk], recv_sem=h_recv.at[d, r, chunk],
+            device_id=(u, right if d == 0 else left), device_id_type=MESH)
+
+    def far_half(r, chunk):
+        return pltpu.make_async_remote_copy(
+            src_ref=kv.at[1, r, chunk, 1], dst_ref=passing.at[r, chunk],
+            send_sem=c_send.at[r, chunk], recv_sem=r_recv.at[r, chunk],
+            device_id=(u, relay), device_id_type=MESH)
+
+    def forward(r, chunk):
+        return pltpu.make_async_remote_copy(
+            src_ref=passing.at[r, chunk], dst_ref=kv.at[beyond_column, r, chunk, 1],
+            send_sem=r_send.at[r, chunk], recv_sem=c_recv.at[r, chunk],
+            device_id=(u, beyond), device_id_type=MESH)
+
+    def far_arrival(r, chunk):
+        return pltpu.make_async_remote_copy(
+            src_ref=passing.at[r, chunk], dst_ref=kv.at[far_column, r, chunk, 1],
+            send_sem=r_send.at[r, chunk], recv_sem=c_recv.at[r, chunk],
+            device_id=(u, beyond), device_id_type=MESH)
+
+    def h_start(r, chunk):
+        for d, there, wide in ((0, has_right, w == 3), (1, has_left, w == 4)):
+            @pl.when(there & ~wide)
+            def _():
+                h_copy(d, r, chunk).start()
+
+            @pl.when(wide)
+            def _():
+                far_half(r, chunk).start()
+                near_half(d, r, chunk).start()
+
+    def h_arrive(r, chunk):
+        for d, there, wide in ((0, has_left, w == 4), (1, has_right, w == 3)):
+            @pl.when(there & ~wide)
+            def _():
+                h_copy(d, r, chunk).wait_recv()
+
+            @pl.when(wide)
+            def _():
+                near_half(d, r, chunk).wait_recv()
+                far_arrival(r, chunk).wait_recv()
+
+    def h_sent(r, chunk):
+        for d, there, wide in ((0, has_right, w == 3), (1, has_left, w == 4)):
+            @pl.when(there & ~wide)
+            def _():
+                h_copy(d, r, chunk).wait_send()
+
+            @pl.when(wide)
+            def _():
+                far_half(r, chunk).wait_send()
+                near_half(d, r, chunk).wait_send()
+
+        @pl.when(relays)
+        def _():
+            forward(r, chunk).wait_send()
+
+    def rows(action, chunk, which=(0, 1, 2)):
+        for r in which:
+            if r == 1:
+                action(r, chunk)
+            else:
+                pl.when(has_row[r])(functools.partial(action, r, chunk))
+
+    def pass_on(r, chunk):
+        @pl.when(relays)
+        def _():
+            far_half(r, chunk).wait_recv()
+            forward(r, chunk).start()
+
     def o_dst(frame, head):
         return out_hbm.at[pl.ds(pl.multiple_of(frame % 2 * TILE, TILE), TILE),
                           pl.ds(pl.multiple_of(head * HD, HD), HD)]
@@ -131,7 +221,7 @@
                     q, near(c, r, 0), (((1,), (1,)), ((), ())),
                     preferred_element_type=jnp.float32)
                 for a in range(3):
-                    bias = jnp.where(live[f * 27 + 9 * a + 3 * r + c] > 0, 0.0, NEG)
+                    bias = jnp.where(live[0, f, 0, 9 * a + 3 * r + c] > 0, 0.0, NEG)
                     part = scores[:, a * TILE:(a + 1) * TILE] * LOGIT + bias
                     sc[3 * r + c, :, a * TILE:(a + 1) * TILE] = part
                     top = jnp.maximum(top, part)
@@ -183,13 +273,7 @@
             def _():
                 v_copy(1, c).start()
 
-            @pl.when(has_right)
-            def _():
-                h_copy(0, 1, c).start()
-
-            @pl.when(has_left)
-            def _():
-                h_copy(1, 1, c).start()
+            h_start(1, c)
 
         @pl.when((i >= LAG_V) & (i < N + LAG_V))
         def _():
@@ -198,25 +282,16 @@
                 @pl.when(there)
                 def _():
                     v_copy(d, c).wait_recv()
-
-                    @pl.when(has_right)
-                    def _():
-                        h_copy(0, r, c).start()
-
-                    @pl.when(has_left)
-                    def _():
-                        h_copy(1, r, c).start()
+                    h_start(r, c)
+
+        @pl.when((i >= LAG_R) & (i < N + LAG_R))
+        def _():
+            rows(pass_on, (u + i + N - LAG_R) % N, (1, 0, 2))
 
         @pl.when(i >= LAG_H)
         def _():
             c = (u + i + N - LAG_H) % N
-            for d, there in ((0, has_left), (1, has_right)):
-                for r in range(3):
-                    here = there if r == 1 else there & has_row[r]
-
-                    @pl.when(here)
-                    def _():
-                        h_copy(d, r, c).wait_recv()
+            rows(h_arrive, c)
             wait_a(2, c)
 
             @pl.when(i > LAG_H)
@@ -235,13 +310,7 @@
         def _():
             v_copy(1, g).wait_send()
 
-        for d, there in ((0, has_right), (1, has_left)):
-            for r in range(3):
-                here = there if r == 1 else there & has_row[r]
-
-                @pl.when(here)
-                def _():
-                    h_copy(d, r, g).wait_send()
+        rows(h_sent, g)
 
         @pl.when(g != u)
         def _():
@@ -270,14 +339,16 @@
             pltpu.VMEM((N, 2 * TILE, HD), jnp.bfloat16),
             pltpu.VMEM((FRAMES, TILE, HD), jnp.bfloat16),
             pltpu.VMEM((9, TILE, 3 * TILE), jnp.float32),
+            pltpu.VMEM((3, N, 2 * TILE, HD), jnp.bfloat16),
             DMA((3, N)), DMA((3, N)),
             DMA((2, N)), DMA((2, N)),
             DMA((2, 3, N)), DMA((2, 3, N)),
+            DMA((3, N)), DMA((3, N)), DMA((3, N)), DMA((3, N)),
             DMA((FRAMES,)), DMA((N, 2)),
         ],
         compiler_params=pltpu.CompilerParams(
-            collective_id=0, has_side_effects=True, vmem_limit_bytes=48 << 20),
-    )(query, key, value, live.reshape(-1))
+            collective_id=0, has_side_effects=True, vmem_limit_bytes=62 << 20),
+    )(query, key, value, live)
 
 
 def solution(mesh):

time: 112 us -> 92.7 us (0.83)
  the two profiles are of different devices: /device:TPU:113 before, /device:TPU:75 now
where the time goes in v2:
time: 92.7 us; the launch traced here: 92.4 us
  Pallas kernels  90.6 us (98%)
  local copies, waits for them, and re-layouts  1.87 us (2%)
    pallas_call x1, Pallas kernels, local(): pl.pallas_call(kernel, out_shape=jax.ShapeDtypeStruct((rows, width), jnp....  90.6 us
    unnamed x1, local copies, waits for them, and re-layouts  1.87 us

profile of v2, /device:TPU:75, one launch (start us, length us, event | category | flops | bytes accessed | tf_op | source)
XLA Modules:
  0.0 92.4 jit_solution(16303877001533729546)
XLA Ops:
  0.0 90.6 %shard_map.46 = bf16[256,1024]{1,0:T(8,128)(2,1)} custom-call(bf16[256,1024]{1,0:T(8,128)(2,1)} %q_hbm.1, bf16[256,1024]{1,0:T(8,128)(2,1)} %k_hbm.1, bf16[256,1024]{1,0:T(8,128)(2,1)} %v_hbm.1, s32[1,16,1,27]{3,2,1,0:T(1,128)} %live.1), custom_call_target="tpu_custom_call" | custom-call | tf_op jit(solution)/shard_map/pallas_call | solution.py:332
  90.6 1.9 %copy.6 = bf16[256,1024]{1,0:T(8,128)(2,1)} copy(bf16[256,1024]{1,0:T(8,128)(2,1)} %shard_map.46) | data formatting | bytes 1048576

commit v3 on v1

v3 whole, which is shorter than its diff:
```python
import functools
import math

import jax
import jax.numpy as jnp
from jax import lax
from jax.experimental import pallas as pl
from jax.experimental.pallas import tpu as pltpu
from jax.sharding import PartitionSpec as P

HD = 128
TILE = 128
TW = 8
TH = 8
N = 8
FRAMES = 2 * N
LAG_V = 1
LAG_R = 2
LAG_H = 3
DIRECT = 2
LOGIT = HD ** (-0.5) * math.log2(math.e)
NEG = -1e30
MESH = pl.DeviceIdType.MESH
DMA = pltpu.SemaphoreType.DMA


def kernel(
    q_hbm, k_hbm, v_hbm, live_hbm, out_hbm,
    kv, qb, ob, sc, passing, live_in, live,
    a_send, a_recv, v_send, v_recv, h_send, h_recv, c_send, c_recv, r_send, r_recv, o_send, o_recv,
    l_send, l_recv,
):
    pu = lax.axis_index("uly")
    ps = lax.axis_index("blk")
    odd = ps // 4 % 2
    rx = (pu // 4 * 2 + ps // 2 % 2 + 4 - odd) % 4
    u = rx // 2 * 4 + pu % 4
    s = ps // 4 * 4 + rx % 2 * 2 + ps % 2
    even = odd == 0

    def place(head, tile):
        z = tile // 4
        x = (head // 4 * 2 + tile // 2 % 2 + z % 2) % 4
        return (x // 2 * 4 + head % 4, z * 4 + x % 2 * 2 + tile % 2)

    h = s // TW
    w = s % TW
    up = ((h + 1) % TH) * TW + w
    down = ((h + TH - 1) % TH) * TW + w
    right = h * TW + (w + 1) % TW
    left = h * TW + (w + TW - 1) % TW
    has_up, has_down = h < TH - 1, h > 0
    has_right, has_left = w < TW - 1, w > 0
    has_row = (has_down, None, has_up)
    crosses = (w == 3) | (w == 4)
    relays = (w == 1) | (w == 6)
    relay = h * TW + jnp.where(w == 3, 1, 6)
    beyond = h * TW + jnp.where(w == 1, 4, 3)
    beyond_column = jnp.where(w == 1, 0, 2)
    far_column = jnp.where(w == 3, 2, 0)

    extra = crosses | relays
    barrier = pltpu.get_barrier_semaphore()

    def greet(head, tile):
        pl.semaphore_signal(barrier, inc=1, device_id=place(head, tile), device_id_type=MESH)

    for i in range(1, N):
        greet((pu + i) % N, ps)
    for other in (up, down, left, right):
        greet(u, other)

    @pl.when(odd == 1)
    def _():
        greet(pu, ps)

    @pl.when(extra)
    def _():
        for a, b in ((1, 3), (6, 4)):
            other = h * TW + jnp.where(crosses, a, b)
            greet(u, other)
            greet((u + 4) % N, other)


    def columns(ref, head):
        return ref.at[:, pl.ds(pl.multiple_of(head * HD, HD), HD)]

    def a_dst(x, chunk):
        return qb.at[chunk] if x == 2 else kv.at[1, 1, chunk, x]

    def a_copy(x, to):
        ref = (k_hbm, v_hbm, q_hbm)[x]
        return pltpu.make_async_remote_copy(
            src_ref=columns(ref, to), dst_ref=a_dst(x, pu),
            send_sem=a_send.at[x, to], recv_sem=a_recv.at[x, pu],
            device_id=place(to, ps), device_id_type=MESH)

    def a_own(x):
        ref = (k_hbm, v_hbm, q_hbm)[x]
        return pltpu.make_async_copy(columns(ref, u), a_dst(x, u), a_recv.at[x, u])

    def live_copy():
        return pltpu.make_async_remote_copy(
            src_ref=live_hbm, dst_ref=live_in, send_sem=l_send, recv_sem=l_recv,
            device_id=place(pu, ps), device_id_type=MESH)

    def live_own():
        return pltpu.make_async_copy(live_hbm, live_in, l_recv)

    @pl.when(even)
    def _():
        for x in (0, 1, 2):
            a_own(x).start()
        live_own().start()

    def zero(*at):
        @pl.loop(0, N)
        def _(g):
            for part in range(2):
                kv[(*at, g, part)] = jnp.zeros((2 * TILE, HD), jnp.bfloat16)

    for missing, spots in (
        (h == 0, [(c, 0) for c in range(3)]),
        (h == TH - 1, [(c, 2) for c in range(3)]),
        (w == 0, [(0, r) for r in range(3)]),
        (w == TW - 1, [(2, r) for r in range(3)]),
    ):
        @pl.when(missing)
        def _():
            for spot in spots:
                zero(*spot)

    pl.semaphore_wait(barrier, N + 3 + odd + 4 * extra.astype(jnp.int32))

    @pl.when(odd == 1)
    def _():
        for x in (0, 1):
            a_copy(x, pu).start()

    for xs in ((0, 1), (2,)):
        @pl.loop(1, N)
        def _(i):
            to = (pu + N - i) % N
            for x in xs:
                a_copy(x, to).start()

    @pl.when(odd == 1)
    def _():
        a_copy(2, pu).start()
        live_copy().start()

    def v_copy(d, chunk):
        return pltpu.make_async_remote_copy(
            src_ref=kv.at[1, 1, chunk], dst_ref=kv.at[1, 0 if d == 0 else 2, chunk],
            send_sem=v_send.at[d, chunk], recv_sem=v_recv.at[d, chunk],
            device_id=place(u, up if d == 0 else down), device_id_type=MESH)

    def h_copy(d, r, chunk):
        return pltpu.make_async_remote_copy(
            src_ref=kv.at[1, r, chunk], dst_ref=kv.at[0 if d == 0 else 2, r, chunk],
            send_sem=h_send.at[d, r, chunk], recv_sem=h_recv.at[d, r, chunk],
            device_id=place(u, right if d == 0 else left), device_id_type=MESH)

    def near_half(d, r, chunk):
        return pltpu.make_async_remote_copy(
            src_ref=kv.at[1, r, chunk, 0], dst_ref=kv.at[0 if d == 0 else 2, r, chunk, 0],
            send_sem=h_send.at[d, r, chunk], recv_sem=h_recv.at[d, r, chunk],
            device_id=place(u, right if d == 0 else left), device_id_type=MESH)

    def via(chunk):
        return jnp.where(chunk % 2 == 0, u, (u + 4) % N)

    def far_half(r, chunk):
        return pltpu.make_async_remote_copy(
            src_ref=kv.at[1, r, chunk, 1], dst_ref=passing.at[r, chunk],
            send_sem=c_send.at[r, chunk], recv_sem=r_recv.at[r, chunk],
            device_id=place(via(chunk), relay), device_id_type=MESH)

    def forward(r, chunk):
        return pltpu.make_async_remote_copy(
            src_ref=passing.at[r, chunk], dst_ref=kv.at[beyond_column, r, chunk, 1],
            send_sem=r_send.at[r, chunk], recv_sem=c_recv.at[r, chunk],
            device_id=place(via(chunk), beyond), device_id_type=MESH)

    def far_arrival(r, chunk):
        return pltpu.make_async_remote_copy(
            src_ref=passing.at[r, chunk], dst_ref=kv.at[far_column, r, chunk, 1],
            send_sem=r_send.at[r, chunk], recv_sem=c_recv.at[r, chunk],
            device_id=place(via(chunk), beyond), device_id_type=MESH)

    def late(chunk):
        return (chunk + N - u) % N >= N - DIRECT

    def late_by(chunk):
        return (chunk + N - via(chunk)) % N >= N - DIRECT

    def h_start(r, chunk):
        for d, there, wide in ((0, has_right, (w == 3) & ~late(chunk)), (1, has_left, (w == 4) & ~late(chunk))):
            @pl.when(there & ~wide)
            def _():
                h_copy(d, r, chunk).start()

            @pl.when(wide)
            def _():
                far_half(r, chunk).start()
                near_half(d, r, chunk).start()

    def h_arrive(r, chunk):
        for d, there, wide in ((0, has_left, (w == 4) & ~late(chunk)), (1, has_right, (w == 3) & ~late(chunk))):
            @pl.when(there & ~wide)
            def _():
                h_copy(d, r, chunk).wait_recv()

            @pl.when(wide)
            def _():
                near_half(d, r, chunk).wait_recv()
                far_arrival(r, chunk).wait_recv()

    def h_sent(r, chunk):
        for d, there, wide in ((0, has_right, (w == 3) & ~late(chunk)), (1, has_left, (w == 4) & ~late(chunk))):
            @pl.when(there & ~wide)
            def _():
                h_copy(d, r, chunk).wait_send()

            @pl.when(wide)
            def _():
                far_half(r, chunk).wait_send()
                near_half(d, r, chunk).wait_send()

        @pl.when(relays & ~late_by(chunk))
        def _():
            forward(r, chunk).wait_send()

    def rows(action, chunk, which=(0, 1, 2)):
        for r in which:
            if r == 1:
                action(r, chunk)
            else:
                pl.when(has_row[r])(functools.partial(action, r, chunk))

    def pass_on(r, chunk):
        @pl.when(relays & ~late_by(chunk))
        def _():
            far_half(r, chunk).wait_recv()
            forward(r, chunk).start()

    def o_dst(frame, head):
        return out_hbm.at[pl.ds(pl.multiple_of(frame % 2 * TILE, TILE), TILE),
                          pl.ds(pl.multiple_of(head * HD, HD), HD)]

    def o_copy(frame):
        return pltpu.make_async_remote_copy(
            src_ref=ob.at[frame], dst_ref=o_dst(frame, u),
            send_sem=o_send.at[frame], recv_sem=o_recv.at[u, frame % 2],
            device_id=(frame // 2, s), device_id_type=MESH)

    def o_own(frame):
        return pltpu.make_async_copy(ob.at[frame], o_dst(frame, u), o_send.at[frame])

    def attend(f):
        q = qb[f // 2, pl.ds(pl.multiple_of(f % 2 * TILE, TILE), TILE), :]
        spots = []
        for a in range(3):
            g = (f + a + FRAMES - 1) % FRAMES
            spots.append((g // 2, pl.multiple_of(g % 2 * TILE, TILE)))

        def near(c, r, part):
            return jnp.concatenate(
                [kv[c, r, g, part, pl.ds(off, TILE), :] for g, off in spots], axis=0)

        top = jnp.full((TILE, TILE), NEG, jnp.float32)
        for r in range(3):
            for c in range(3):
                scores = lax.dot_general(
                    q, near(c, r, 0), (((1,), (1,)), ((), ())),
                    preferred_element_type=jnp.float32)
                for a in range(3):
                    bias = jnp.where(live[0, f, 0, 9 * a + 3 * r + c] > 0, 0.0, NEG)
                    part = scores[:, a * TILE:(a + 1) * TILE] * LOGIT + bias
                    sc[3 * r + c, :, a * TILE:(a + 1) * TILE] = part
                    top = jnp.maximum(top, part)
        top = jnp.max(top, axis=1, keepdims=True)
        total = jnp.zeros((TILE, TILE), jnp.float32)
        mixed = jnp.zeros((TILE, HD), jnp.float32)
        for r in range(3):
            for c in range(3):
                weights = jnp.exp2(sc[3 * r + c] - top)
                for a in range(3):
                    total += weights[:, a * TILE:(a + 1) * TILE]
                mixed += jnp.dot(
                    weights.astype(jnp.bfloat16), near(c, r, 1),
                    preferred_element_type=jnp.float32)
        ob[f] = (mixed / jnp.sum(total, axis=1, keepdims=True)).astype(jnp.bfloat16)

    def attend_and_send(f):
        attend(f)

        @pl.when(even & (f // 2 == u))
        def _():
            o_own(f).start()

        @pl.when((odd == 1) | (f // 2 != u))
        def _():
            o_copy(f).start()

    def unit(c):
        @pl.loop(0, 2)
        def _(j):
            attend_and_send((2 * c + j + FRAMES - 1) % FRAMES)

    def wait_a(x, chunk):
        pltpu.make_async_copy(columns(k_hbm, 0), a_dst(x, chunk), a_recv.at[x, chunk]).wait()

    @pl.loop(0, N + LAG_H)
    def _(i):
        @pl.when(i < N)
        def _():
            c = (u + i) % N
            wait_a(0, c)
            wait_a(1, c)

            @pl.when(has_up)
            def _():
                v_copy(0, c).start()

            @pl.when(has_down)
            def _():
                v_copy(1, c).start()

            h_start(1, c)

        @pl.when((i >= LAG_V) & (i < N + LAG_V))
        def _():
            c = (u + i + N - LAG_V) % N
            for d, r, there in ((0, 0, has_down), (1, 2, has_up)):
                @pl.when(there)
                def _():
                    v_copy(d, c).wait_recv()
                    h_start(r, c)

        @pl.when((i >= LAG_R) & (i < N + LAG_R))
        def _():
            c = (u + i + N - LAG_R) % N
            rows(pass_on, jnp.where(c % 2 == 0, c, (c + 4) % N), (1, 0, 2))

        @pl.when(i == LAG_H)
        def _():
            live_own().wait()
            pltpu.sync_copy(live_in, live)

        @pl.when(i >= LAG_H)
        def _():
            c = (u + i + N - LAG_H) % N
            rows(h_arrive, c)
            wait_a(2, c)

            @pl.when(i > LAG_H)
            def _():
                unit(c)

    unit(u)

    @pl.when(odd == 1)
    def _():
        live_copy().wait_send()

    @pl.loop(0, N)
    def _(g):
        @pl.when(has_up)
        def _():
            v_copy(0, g).wait_send()

        @pl.when(has_down)
        def _():
            v_copy(1, g).wait_send()

        rows(h_sent, g)

        @pl.when((odd == 1) | (g != u))
        def _():
            for x in range(3):
                a_copy(x, g).wait_send()
            for j in range(2):
                o_copy(2 * g + j).wait_send()
                pltpu.make_async_copy(ob.at[j], o_dst(j, g), o_recv.at[g, j]).wait()

        @pl.when(even & (g == u))
        def _():
            for j in range(2):
                o_own(2 * g + j).wait()


def local(query, key, value, live):
    rows, width = query.shape
    hbm = pl.BlockSpec(memory_space=pl.ANY)
    return pl.pallas_call(
        kernel,
        out_shape=jax.ShapeDtypeStruct((rows, width), jnp.bfloat16),
        in_specs=[hbm] * 4,
        out_specs=hbm,
        scratch_shapes=[
            pltpu.VMEM((3, 3, N, 2, 2 * TILE, HD), jnp.bfloat16),
            pltpu.VMEM((N, 2 * TILE, HD), jnp.bfloat16),
            pltpu.VMEM((FRAMES, TILE, HD), jnp.bfloat16),
            pltpu.VMEM((9, TILE, 3 * TILE), jnp.float32),
            pltpu.VMEM((3, N, 2 * TILE, HD), jnp.bfloat16),
            pltpu.VMEM(live.shape, jnp.int32), pltpu.SMEM(live.shape, jnp.int32),
            DMA((3, N)), DMA((3, N)),
            DMA((2, N)), DMA((2, N)),
            DMA((2, 3, N)), DMA((2, 3, N)),
            DMA((3, N)), DMA((3, N)), DMA((3, N)), DMA((3, N)),
            DMA((FRAMES,)), DMA((N, 2)),
            DMA, DMA,
        ],
        compiler_params=pltpu.CompilerParams(
            collective_id=0, has_side_effects=True, vmem_limit_bytes=53 << 20),
    )(query, key, value, live)


def solution(mesh):
    return jax.shard_map(
        local,
        mesh=mesh,
        in_specs=(
            P(("uly", "blk"), None),
            P(("uly", "blk"), None),
            P(("uly", "blk"), None),
            P("uly", None, "blk", None),
        ),
        out_specs=P(("uly", "blk"), None),
        check_vma=False,
    )
```

time: 112 us -> 89.9 us (0.80)
  the two profiles are of different devices: /device:TPU:113 before, /device:TPU:120 now
where the time goes in v3:
time: 89.9 us; the launch traced here: 89.8 us
  Pallas kernels  88.3 us (98%)
  local copies, waits for them, and re-layouts  1.49 us (2%)
    pallas_call x1, Pallas kernels, local(): pl.pallas_call(kernel, out_shape=jax.ShapeDtypeStruct((rows, width), jnp....  88.3 us

profile of v3, /device:TPU:120, one launch (start us, length us, event | category | flops | bytes accessed | tf_op | source)
XLA Modules:
  0.0 89.8 jit_solution(4019830983577892779)
XLA Ops:
  0.0 0.0 copy-start
  0.0 0.7 copy-done
  0.7 88.3 %shard_map.46 = bf16[256,1024]{1,0:T(8,128)(2,1)S(1)} custom-call(bf16[256,1024]{1,0:T(8,128)(2,1)} %q_hbm.1, bf16[256,1024]{1,0:T(8,128)(2,1)} %k_hbm.1, bf16[256,1024]{1,0:T(8,128)(2,1)} %v_hbm.1, s32[1,16,1,27]{3,2,1,0:T(1,128)S(1)} %copy-done), custom_call_target="tpu_custom_call" | custom-call | tf_op jit(solution)/shard_map/pallas_call | solution.py:396
  89.0 0.8 copy.6
Async XLA Ops:
  0.0 0.7 copy-start

commit v4 on v3

--- a/solution.py
+++ b/solution.py
@@ -14,9 +14,9 @@
 TH = 8
 N = 8
 FRAMES = 2 * N
-LAG_V = 1
-LAG_R = 2
-LAG_H = 3
+LAG_V = 2
+LAG_R = 3
+LAG_H = 4
 DIRECT = 2
 LOGIT = HD ** (-0.5) * math.log2(math.e)
 NEG = -1e30

time: 89.9 us -> 89.6 us (level)
  the two profiles are of different devices: /device:TPU:120 before, /device:TPU:71 now
where the time goes in v4:
time: 89.6 us; the launch traced here: 89.5 us
  Pallas kernels  88 us (98%)
  local copies, waits for them, and re-layouts  1.49 us (2%)
    pallas_call x1, Pallas kernels, local(): pl.pallas_call(kernel, out_shape=jax.ShapeDtypeStruct((rows, width), jnp....  88 us

profile of v4, /device:TPU:71, one launch (start us, length us, event | category | flops | bytes accessed | tf_op | source)
XLA Modules:
  0.0 89.5 jit_solution(9566014428747403632)
XLA Ops:
  0.0 0.0 copy-start
  0.0 0.7 copy-done
  0.7 88.0 %shard_map.46 = bf16[256,1024]{1,0:T(8,128)(2,1)S(1)} custom-call(bf16[256,1024]{1,0:T(8,128)(2,1)} %q_hbm.1, bf16[256,1024]{1,0:T(8,128)(2,1)} %k_hbm.1, bf16[256,1024]{1,0:T(8,128)(2,1)} %v_hbm.1, s32[1,16,1,27]{3,2,1,0:T(1,128)S(1)} %copy-done), custom_call_target="tpu_custom_call" | custom-call | tf_op jit(solution)/shard_map/pallas_call | solution.py:396
  88.7 0.8 copy.6
Async XLA Ops:
  0.0 0.7 copy-start

commit v5 on v3

--- a/solution.py
+++ b/solution.py
@@ -319,6 +319,8 @@
             wait_a(0, c)
             wait_a(1, c)
 
+            h_start(1, c)
+
             @pl.when(has_up)
             def _():
                 v_copy(0, c).start()
@@ -326,8 +328,6 @@
             @pl.when(has_down)
             def _():
                 v_copy(1, c).start()
-
-            h_start(1, c)
 
         @pl.when((i >= LAG_V) & (i < N + LAG_V))
         def _():

time: 89.9 us -> 91.5 us (1.018)
  the two profiles are of different devices: /device:TPU:120 before, /device:TPU:32 now
where the time goes in v5:
time: 91.5 us; the launch traced here: 91.4 us
  Pallas kernels  89.9 us (98%)
  local copies, waits for them, and re-layouts  1.49 us (2%)
    pallas_call x1, Pallas kernels, local(): pl.pallas_call(kernel, out_shape=jax.ShapeDtypeStruct((rows, width), jnp....  89.9 us

profile of v5, /device:TPU:32, one launch (start us, length us, event | category | flops | bytes accessed | tf_op | source)
XLA Modules:
  0.0 91.4 jit_solution(11290443653732820789)
XLA Ops:
  0.0 0.0 copy-start
  0.0 0.7 copy-done
  0.7 89.9 %shard_map.46 = bf16[256,1024]{1,0:T(8,128)(2,1)S(1)} custom-call(bf16[256,1024]{1,0:T(8,128)(2,1)} %q_hbm.1, bf16[256,1024]{1,0:T(8,128)(2,1)} %k_hbm.1, bf16[256,1024]{1,0:T(8,128)(2,1)} %v_hbm.1, s32[1,16,1,27]{3,2,1,0:T(1,128)S(1)} %copy-done), custom_call_target="tpu_custom_call" | custom-call | tf_op jit(solution)/shard_map/pallas_call | solution.py:396
  90.6 0.8 copy.6
Async XLA Ops:
  0.0 0.7 copy-start
